TPU v7x, 32 devices: a whole 2x2x4 slice. The times are simulated.
32 devices in a mesh: dom: 2 (over x), frame: 16 (over z, y, core).
Axes of the slice: x: 2, y: 2, z: 4, core: 2. Of those that a mesh axis runs over, the one named last changes fastest.
Arguments:
- queries: bfloat16 [32, 512, 1024], P(('dom', 'frame')), parts along dimension 0, may hold values from -8 to 8
- keys: bfloat16 [32, 512, 1024], P(('dom', 'frame')), parts along dimension 0, may hold values from -8 to 8
- values: bfloat16 [32, 512, 1024], P(('dom', 'frame')), parts along dimension 0, may hold values from -6 to 6
- grad_out: bfloat16 [32, 512, 1024], P(('dom', 'frame')), parts along dimension 0, may hold values from -6 to 6
- links: int32 [32, 4], P(('dom', 'frame')), parts along dimension 0, may hold values from 0 to 1, as said below
- w_query: bfloat16 [1024, 1024], replicated, may hold values from -0.1875 to 0.1875
- w_key: bfloat16 [1024, 1024], replicated, may hold values from -0.1875 to 0.1875
- w_value: bfloat16 [1024, 1024], replicated, may hold values from -0.1875 to 0.1875
Outputs:
- grad_input: bfloat16 [32, 512, 1024], P(('dom', 'frame')), parts along dimension 0
There are 2 independent parts, one for each index of `dom`. A program takes and returns all parts, laid end to end along the dimension named above; an argument that names none is the same for every part. Nothing has to cross between parts.
Inputs may be any that keep to these rules, and one draw needn't show every extreme that they name: links[t, j] is 0 whenever t < 2**j; otherwise 0 or 1, so frames attend to ragged numbers of up to 4 earlier frames.
All inputs are finite; a program needn't handle non-finite values.
Results may differ from a plain program's by a relative error of at most 0.0049.
Values may be sent and summed in bfloat16 or wider, within the bound.
A program may use at most 128 MiB of HBM per device.

v0:
```python
import jax
import jax.numpy as jnp
from jax import lax
from jax.sharding import PartitionSpec as P

HEADS = 16
NDIL = 4


def from_behind(block, axis, distance):
    devices = range(lax.axis_size(axis))
    route = [(i - distance, i) for i in devices if i - distance in devices]
    return lax.ppermute(block, axis, route)


def attention_core(query_f, grad_f, key_list, value_list, live_list, score_scale):
    live_mask = jnp.stack([m[:, None, None] for m in live_list])
    scores = jnp.stack([jnp.sum(query_f * k, axis=-1) for k in key_list]) * score_scale
    scores = jnp.where(live_mask > 0, scores, -1e30)
    highest = jnp.max(scores, axis=0)
    weights_raw = jnp.exp(scores - highest) * live_mask
    probability = weights_raw / jnp.sum(weights_raw, axis=0)
    grad_prob = jnp.stack([jnp.sum(grad_f * v, axis=-1) for v in value_list])
    inner_sum = jnp.sum(probability * grad_prob, axis=0)
    grad_score = probability * (grad_prob - inner_sum) * score_scale
    grad_query = jnp.zeros_like(query_f)
    grad_keys = []
    grad_values = []
    for i in range(len(key_list)):
        grad_query = grad_query + grad_score[i][..., None] * key_list[i]
        grad_keys.append(grad_score[i][..., None] * query_f)
        grad_values.append(probability[i][..., None] * grad_f)
    return (grad_query, grad_keys, grad_values, grad_score, probability)


def dot_transposed(left, weight):
    return lax.dot_general(
        left, weight, (((1,), (1,)), ((), ())), preferred_element_type=jnp.float32
    )


def fetch_pairs(paired, spacing):
    return from_behind(paired, "frame", spacing)


def return_inputs(input_pair, spacing):
    return from_behind(input_pair, "frame", -spacing)


def return_weights(weight_pair, spacing):
    return from_behind(weight_pair, "frame", -spacing)


def per_device(queries, keys, values, grad_out, links, w_query, w_key, w_value):
    frames, patches, model_width = queries.shape
    head_size = model_width // HEADS
    score_scale = head_size ** (-0.5)

    def spread_heads(a):
        return a.astype(jnp.float32).reshape(frames, patches, HEADS, head_size)

    query_f = spread_heads(queries)
    grad_f = spread_heads(grad_out)
    paired = jnp.stack([keys, values])
    key_list = [spread_heads(keys)]
    value_list = [spread_heads(values)]
    live_list = [jnp.ones((frames,), jnp.float32)]
    for j in range(NDIL):
        arrived = fetch_pairs(paired, 2**j)
        key_list.append(spread_heads(arrived[0]))
        value_list.append(spread_heads(arrived[1]))
        live_list.append((links[:, j] > 0).astype(jnp.float32))
    grad_query, grad_keys, grad_values, grad_score, probability = attention_core(
        query_f, grad_f, key_list, value_list, live_list, score_scale
    )
    key_total = grad_keys[0]
    value_total = grad_values[0]
    input_pair = jnp.stack([queries, grad_out])
    for j in range(NDIL):
        weight_pair = jnp.stack([grad_score[j + 1], probability[j + 1]]).reshape(
            2, frames, patches * HEADS
        )
        came_inputs = return_inputs(input_pair, 2**j)
        came_weights = return_weights(weight_pair, 2**j).reshape(2, frames, patches, HEADS)
        key_total = key_total + came_weights[0][..., None] * spread_heads(came_inputs[0])
        value_total = value_total + came_weights[1][..., None] * spread_heads(came_inputs[1])
    flat_rows = frames * patches
    total = dot_transposed(grad_query.reshape(flat_rows, model_width).astype(jnp.bfloat16), w_query)
    total = total + dot_transposed(
        key_total.reshape(flat_rows, model_width).astype(jnp.bfloat16), w_key
    )
    total = total + dot_transposed(
        value_total.reshape(flat_rows, model_width).astype(jnp.bfloat16), w_value
    )
    return total.reshape(frames, patches, model_width).astype(jnp.bfloat16)


def solution(mesh):
    placed = (
        P(("dom", "frame"), None, None),
        P(("dom", "frame"), None, None),
        P(("dom", "frame"), None, None),
        P(("dom", "frame"), None, None),
        P(("dom", "frame"), None),
        P(),
        P(),
        P(),
    )
    return jax.shard_map(
        per_device,
        mesh=mesh,
        in_specs=placed,
        out_specs=P(("dom", "frame"), None, None),
        check_vma=False,
    )
```

profile of v0, /device:TPU:0, one launch (start us, length us, event | category | flops | bytes accessed | tf_op | source)
XLA Modules:
  0.0 281.4 jit_solution(18089176259684921676)
XLA Ops:
  1.7 2.7 copy.35
  4.3 2.7 pad_maximum_fusion
  7.1 6.2 %collective-permute-start.1 = (bf16[2,1,512,1024]{2,3,1,0:T(8,128)(2,1)}, bf16[2,1,512,1024]{2,3,1,0:T(8,128)(2,1)}, u32[]{:S(2)}, u32[]{:S(2)}) collective-permute-start(bf16[2,1,512,1024]{2,3,1,0:T(8,128)(2,1)} %pad_maximum_fusion), channel_id=1, source_target_pairs={{0,2},{1,3},{2,4},{3,5},{4,6},{5,7},{6,8},{7,9},{8,10},{9,11},{10,... | collective-permute-start | bytes 6291464 | tf_op jit(solution)/shard_map/ppermute | solution.py:13
  13.3 3.5 %collective-permute-start.2 = (bf16[2,1,512,1024]{2,3,1,0:T(8,128)(2,1)}, bf16[2,1,512,1024]{2,3,1,0:T(8,128)(2,1)}, u32[]{:S(2)}, u32[]{:S(2)}) collective-permute-start(bf16[2,1,512,1024]{2,3,1,0:T(8,128)(2,1)} %pad_maximum_fusion), channel_id=1, source_target_pairs={{0,4},{1,5},{2,6},{3,7},{4,8},{5,9},{6,10},{7,11},{8,12},{9,13},{1... | collective-permute-start | bytes 6291464 | tf_op jit(solution)/shard_map/ppermute | solution.py:13
  16.8 4.5 %collective-permute-start.3 = (bf16[2,1,512,1024]{2,3,1,0:T(8,128)(2,1)}, bf16[2,1,512,1024]{2,3,1,0:T(8,128)(2,1)}, u32[]{:S(2)}, u32[]{:S(2)}) collective-permute-start(bf16[2,1,512,1024]{2,3,1,0:T(8,128)(2,1)} %pad_maximum_fusion), channel_id=1, source_target_pairs={{0,8},{1,9},{2,10},{3,11},{4,12},{5,13},{6,14},{7,15},{16,24},{17,... | collective-permute-start | bytes 6291464 | tf_op jit(solution)/shard_map/ppermute | solution.py:13
  21.3 2.7 collective-permute-start
  23.9 2.3 copy.32
  27.7 2.7 pad_maximum_fusion.1
  35.2 23.1 %collective-permute-done.1 = bf16[2,1,512,1024]{2,3,1,0:T(8,128)(2,1)} collective-permute-done((bf16[2,1,512,1024]{2,3,1,0:T(8,128)(2,1)}, bf16[2,1,512,1024]{2,3,1,0:T(8,128)(2,1)}, u32[]{:S(2)}, u32[]{:S(2)}) %collective-permute-start.1) | collective-permute-done | bytes 2097184 | tf_op jit(solution)/shard_map/ppermute | solution.py:13
  59.6 1.9 slice_convert_fusion.2
  63.1 1.9 slice_convert_fusion.1
  64.9 40.4 %collective-permute-done.3 = bf16[2,1,512,1024]{2,3,1,0:T(8,128)(2,1)} collective-permute-done((bf16[2,1,512,1024]{2,3,1,0:T(8,128)(2,1)}, bf16[2,1,512,1024]{2,3,1,0:T(8,128)(2,1)}, u32[]{:S(2)}, u32[]{:S(2)}) %collective-permute-start.3) | collective-permute-done | bytes 2097184 | tf_op jit(solution)/shard_map/ppermute | solution.py:13
  106.6 1.9 slice_convert_fusion
  108.6 2.0 slice_convert_fusion.3
  117.1 1.9 reshape.1111
  122.1 1.9 reshape.1112
  125.0 2.0 reshape.1113
  128.0 1.9 reshape.1114
  134.5 54.4 %collective-permute-done.6 = f32[2,1,8192]{2,0,1:T(2,128)} collective-permute-done((f32[2,1,8192]{2,0,1:T(2,128)}, f32[2,1,8192]{2,0,1:T(2,128)}, u32[]{:S(2)}, u32[]{:S(2)}) %collective-permute-start.6) | collective-permute-done | bytes 65568 | tf_op jit(solution)/shard_map/ppermute | solution.py:13
  193.5 46.3 %collective-permute-done.8 = f32[2,1,8192]{2,0,1:T(2,128)} collective-permute-done((f32[2,1,8192]{2,0,1:T(2,128)}, f32[2,1,8192]{2,0,1:T(2,128)}, u32[]{:S(2)}, u32[]{:S(2)}) %collective-permute-start.8) | collective-permute-done | bytes 65568 | tf_op jit(solution)/shard_map/ppermute | solution.py:13
  244.6 13.3 %collective-permute-done.10 = f32[2,1,8192]{2,0,1:T(2,128)} collective-permute-done((f32[2,1,8192]{2,0,1:T(2,128)}, f32[2,1,8192]{2,0,1:T(2,128)}, u32[]{:S(2)}, u32[]{:S(2)}) %collective-permute-start.10) | collective-permute-done | bytes 65568 | tf_op jit(solution)/shard_map/ppermute | solution.py:13
  267.6 5.1 %fusion.9 = (bf16[512,1024]{0,1:T(8,128)(2,1)S(1)}, bf16[512,1024]{0,1:T(8,128)(2,1)S(1)}) fusion(bf16[2,1,512,1024]{2,3,1,0:T(8,128)(2,1)} %collective-permute-done.11, bf16[2,1,512,1024]{2,3,1,0:T(8,128)(2,1)} %collective-permute-done.9, bf16[2,1,512,1024]{2,3,1,0:T(8,128)(2,1)} %collective-permute-done.7, ...), kind=kLoop, calls=%fused_computation.11 | loop fusion | flops 15728640 | bytes 12877824 | tf_op jit(solution)/shard_map/convert_element_type | solution.py:90
  275.8 3.3 %fusion.11 = bf16[512,1024]{0,1:T(8,128)(2,1)S(1)} fusion(bf16[2,1,512,1024]{2,3,1,0:T(8,128)(2,1)} %collective-permute-done.11, bf16[2,1,512,1024]{2,3,1,0:T(8,128)(2,1)} %collective-permute-done.9, bf16[2,1,512,1024]{2,3,1,0:T(8,128)(2,1)} %collective-permute-done.7, bf16[2,1,512,1024]{2,3,1,0:T(8,128)(2,1)} %collective-permute-done.5, ...), kind=kLoop, calls=%fused_computation.16 | loop fusion | flops 7864320 | bytes 6455296 | tf_op jit(solution)/shard_map/convert_element_type | solution.py:93
  279.1 2.3 fusion.20
  (94 shorter events, 47.3 us)
Async XLA Ops:
  0.0 272.8 %copy-start = (bf16[1024,1024]{1,0:T(8,128)(2,1)S(1)}, bf16[1024,1024]{1,0:T(8,128)(2,1)}, u32[]{:S(2)}) copy-start(bf16[1024,1024]{1,0:T(8,128)(2,1)} %param.13) | copy-start | bytes 6291460
  1.7 5.4 %copy-start.1 = (bf16[1,512,1024]{1,2,0:T(8,128)(2,1)}, bf16[1,512,1024]{1,2,0:T(8,128)(2,1)S(1)}, u32[]{:S(2)}) copy-start(bf16[1,512,1024]{1,2,0:T(8,128)(2,1)S(1)} %copy.33) | copy-start | bytes 3145732
  7.1 51.2 %collective-permute-start.1 = (bf16[2,1,512,1024]{2,3,1,0:T(8,128)(2,1)}, bf16[2,1,512,1024]{2,3,1,0:T(8,128)(2,1)}, u32[]{:S(2)}, u32[]{:S(2)}) collective-permute-start(bf16[2,1,512,1024]{2,3,1,0:T(8,128)(2,1)} %pad_maximum_fusion), channel_id=1, source_target_pairs={{0,2},{1,3},{2,4},{3,5},{4,6},{5,7},{6,8},{7,9},{8,10},{9,11},{10,... | collective-permute-start | bytes 6291464 | tf_op jit(solution)/shard_map/ppermute | solution.py:13
  13.3 48.5 %collective-permute-start.2 = (bf16[2,1,512,1024]{2,3,1,0:T(8,128)(2,1)}, bf16[2,1,512,1024]{2,3,1,0:T(8,128)(2,1)}, u32[]{:S(2)}, u32[]{:S(2)}) collective-permute-start(bf16[2,1,512,1024]{2,3,1,0:T(8,128)(2,1)} %pad_maximum_fusion), channel_id=1, source_target_pairs={{0,4},{1,5},{2,6},{3,7},{4,8},{5,9},{6,10},{7,11},{8,12},{9,13},{1... | collective-permute-start | bytes 6291464 | tf_op jit(solution)/shard_map/ppermute | solution.py:13
  16.8 88.6 %collective-permute-start.3 = (bf16[2,1,512,1024]{2,3,1,0:T(8,128)(2,1)}, bf16[2,1,512,1024]{2,3,1,0:T(8,128)(2,1)}, u32[]{:S(2)}, u32[]{:S(2)}) collective-permute-start(bf16[2,1,512,1024]{2,3,1,0:T(8,128)(2,1)} %pad_maximum_fusion), channel_id=1, source_target_pairs={{0,8},{1,9},{2,10},{3,11},{4,12},{5,13},{6,14},{7,15},{16,24},{17,... | collective-permute-start | bytes 6291464 | tf_op jit(solution)/shard_map/ppermute | solution.py:13
  21.3 87.3 %collective-permute-start = (bf16[2,1,512,1024]{2,3,1,0:T(8,128)(2,1)}, bf16[2,1,512,1024]{2,3,1,0:T(8,128)(2,1)}, u32[]{:S(2)}, u32[]{:S(2)}) collective-permute-start(bf16[2,1,512,1024]{2,3,1,0:T(8,128)(2,1)} %pad_maximum_fusion), channel_id=1, source_target_pairs={{0,1},{1,2},{2,3},{3,4},{4,5},{5,6},{6,7},{7,8},{8,9},{9,10},{10,1... | collective-permute-start | bytes 6291464 | tf_op jit(solution)/shard_map/ppermute | solution.py:13
  27.7 4.0 %copy-start.10 = (s32[1,4]{1,0:T(1,128)S(1)}, s32[1,4]{1,0:T(1,128)}, u32[]{:S(2)}) copy-start(s32[1,4]{1,0:T(1,128)} %param.12) | copy-start | bytes 52
  30.4 237.2 %collective-permute-start.11 = (bf16[2,1,512,1024]{2,3,1,0:T(8,128)(2,1)}, bf16[2,1,512,1024]{2,3,1,0:T(8,128)(2,1)}, u32[]{:S(2)}, u32[]{:S(2)}) collective-permute-start(bf16[2,1,512,1024]{2,3,1,0:T(8,128)(2,1)} %pad_maximum_fusion.1), channel_id=1, source_target_pairs={{8,0},{9,1},{10,2},{11,3},{12,4},{13,5},{14,6},{15,7},{24,16},{25,... | collective-permute-start | bytes 6291464 | tf_op jit(solution)/shard_map/ppermute | solution.py:13
  58.3 209.4 %collective-permute-start.5 = (bf16[2,1,512,1024]{2,3,1,0:T(8,128)(2,1)}, bf16[2,1,512,1024]{2,3,1,0:T(8,128)(2,1)}, u32[]{:S(2)}, u32[]{:S(2)}) collective-permute-start(bf16[2,1,512,1024]{2,3,1,0:T(8,128)(2,1)} %pad_maximum_fusion.1), channel_id=1, source_target_pairs={{1,0},{2,1},{3,2},{4,3},{5,4},{6,5},{7,6},{8,7},{9,8},{10,9},{11,1... | collective-permute-start | bytes 6291464 | tf_op jit(solution)/shard_map/ppermute | solution.py:13
  61.8 205.9 %collective-permute-start.7 = (bf16[2,1,512,1024]{2,3,1,0:T(8,128)(2,1)}, bf16[2,1,512,1024]{2,3,1,0:T(8,128)(2,1)}, u32[]{:S(2)}, u32[]{:S(2)}) collective-permute-start(bf16[2,1,512,1024]{2,3,1,0:T(8,128)(2,1)} %pad_maximum_fusion.1), channel_id=1, source_target_pairs={{2,0},{3,1},{4,2},{5,3},{6,4},{7,5},{8,6},{9,7},{10,8},{11,9},{12,... | collective-permute-start | bytes 6291464 | tf_op jit(solution)/shard_map/ppermute | solution.py:13
  105.3 162.3 %collective-permute-start.9 = (bf16[2,1,512,1024]{2,3,1,0:T(8,128)(2,1)}, bf16[2,1,512,1024]{2,3,1,0:T(8,128)(2,1)}, u32[]{:S(2)}, u32[]{:S(2)}) collective-permute-start(bf16[2,1,512,1024]{2,3,1,0:T(8,128)(2,1)} %pad_maximum_fusion.1), channel_id=1, source_target_pairs={{4,0},{5,1},{6,2},{7,3},{8,4},{9,5},{10,6},{11,7},{12,8},{13,9},{1... | collective-permute-start | bytes 6291464 | tf_op jit(solution)/shard_map/ppermute | solution.py:13
  108.5 2.1 copy-start.2
  108.5 2.2 copy-start.3
  110.7 1.9 copy-start.4
  119.1 10.9 %collective-permute-start.4 = (f32[2,1,8192]{2,0,1:T(2,128)}, f32[2,1,8192]{2,0,1:T(2,128)}, u32[]{:S(2)}, u32[]{:S(2)}) collective-permute-start(f32[2,1,8192]{2,0,1:T(2,128)} %reshape.1111), channel_id=1, source_target_pairs={{1,0},{2,1},{3,2},{4,3},{5,4},{6,5},{7,6},{8,7},{9,8},{10,9},{11,1... | collective-permute-start | bytes 196616 | tf_op jit(solution)/shard_map/ppermute | solution.py:13
  130.0 59.0 %collective-permute-start.6 = (f32[2,1,8192]{2,0,1:T(2,128)}, f32[2,1,8192]{2,0,1:T(2,128)}, u32[]{:S(2)}, u32[]{:S(2)}) collective-permute-start(f32[2,1,8192]{2,0,1:T(2,128)} %reshape.1112), channel_id=1, source_target_pairs={{2,0},{3,1},{4,2},{5,3},{6,4},{7,5},{8,6},{9,7},{10,8},{11,9},{12,... | collective-permute-start | bytes 196616 | tf_op jit(solution)/shard_map/ppermute | solution.py:13
  188.9 50.9 %collective-permute-start.8 = (f32[2,1,8192]{2,0,1:T(2,128)}, f32[2,1,8192]{2,0,1:T(2,128)}, u32[]{:S(2)}, u32[]{:S(2)}) collective-permute-start(f32[2,1,8192]{2,0,1:T(2,128)} %reshape.1113), channel_id=1, source_target_pairs={{4,0},{5,1},{6,2},{7,3},{8,4},{9,5},{10,6},{11,7},{12,8},{13,9},{1... | collective-permute-start | bytes 196616 | tf_op jit(solution)/shard_map/ppermute | solution.py:13
  239.8 18.1 %collective-permute-start.10 = (f32[2,1,8192]{2,0,1:T(2,128)}, f32[2,1,8192]{2,0,1:T(2,128)}, u32[]{:S(2)}, u32[]{:S(2)}) collective-permute-start(f32[2,1,8192]{2,0,1:T(2,128)} %reshape.1114), channel_id=1, source_target_pairs={{8,0},{9,1},{10,2},{11,3},{12,4},{13,5},{14,6},{15,7},{24,16},{25,... | collective-permute-start | bytes 196616 | tf_op jit(solution)/shard_map/ppermute | solution.py:13
  272.8 1.6 copy-start.11
  274.4 1.4 copy-start.6
  274.4 1.4 copy-start.7
  274.4 1.4 copy-start.8
  274.4 1.4 copy-start.9
  275.8 3.3 %copy-start.12 = (bf16[1024,1024]{1,0:T(8,128)(2,1)S(1)}, bf16[1024,1024]{1,0:T(8,128)(2,1)}, u32[]{:S(2)}) copy-start(bf16[1024,1024]{1,0:T(8,128)(2,1)} %param.15) | copy-start | bytes 6291460
  (1 other events, 1.3 us)
where the time goes:
time: 283 us; the launch traced here: 281 us
  waiting for transfers between devices  178 us (63%)
  local copies, waits for them, and re-layouts  41.9 us (15%)
  starting transfers between devices  27.3 us (10%)
  other arithmetic  26.3 us (9%)
  matrix products  4.93 us (2%)
  between operations  3.09 us (1%)
    ppermute x12, waiting for transfers between devices, from_behind(): return lax.ppermute(block, axis, route)  178 us
    ppermute x12, starting transfers between devices, from_behind(): return lax.ppermute(block, axis, route)  27.3 us
    unnamed x38, local copies, waits for them, and re-layouts  8.54 us
    reshape x4, local copies, waits for them, and re-layouts, per_device(): jnp.stack([grad_score[j + 1], probability[j + 1]])  7.8 us
    convert_element_type x4, other arithmetic, spread_heads(): return a.astype(jnp.float32).reshape(frames, patches, HEADS, head_size)  7.68 us
    slice x4, local copies, waits for them, and re-layouts, per_device(): came_weights[0][..., None] * spread_heads(came_inputs[0])  6.82 us
    mul x8, local copies, waits for them, and re-layouts, per_device(): came_weights[0][..., None] * spread_heads(came_inputs[0])  6.35 us
    mul x8, local copies, waits for them, and re-layouts, per_device(): came_weights[1][..., None] * spread_heads(came_inputs[1])  6.34 us
  transfers between devices with their start and end apart: 12, of which 6 were waited for; matrix products, arithmetic and copies ran while one was open for 19% of the time, Pallas kernels for 0%

commit v1 on v0

v1 whole, which is shorter than its diff:
```python
import functools

import jax
import jax.numpy as jnp
from jax import lax
from jax.experimental import pallas as pl
from jax.experimental.pallas import tpu as pltpu
from jax.sharding import PartitionSpec as P

HEADS = 16
NDIL = 4
LANES = 128
AHEAD = 3


def dot_nt(left, right):
    return lax.dot_general(
        left, right, (((1,), (1,)), ((), ())), preferred_element_type=jnp.float32
    )


def dot_nn(left, right):
    return lax.dot_general(
        left, right, (((1,), (0,)), ((), ())), preferred_element_type=jnp.float32
    )


def kernel(n, chunks, rows, links_ref, q_ref, k_ref, v_ref, g_ref, wq_ref, wk_ref, wv_ref,
           out_ref, own, slots, msg_out, msg_in, prods, gather, spread, weights,
           own_sem, w_sem, send_sem, recv_sem, msg_send, msg_recv):
    width = q_ref.shape[-1]
    head = width // HEADS
    scale = head ** (-0.5)
    half = rows // 2
    i = lax.axis_index("frame")
    f32, bf16 = jnp.float32, jnp.bfloat16

    def place(stream):
        return (i, 1) if stream == 0 else (n - 1 - i, -1)

    def load(stream, part, c):
        src = ((k_ref, v_ref), (q_ref, g_ref))[stream][part]
        return pltpu.make_async_copy(
            src.at[0, pl.ds(pl.multiple_of(c * rows, rows), rows), :],
            own.at[stream, c, part], own_sem.at[stream, part, c])

    def hop(stream, kind, c):
        m, sign = place(stream)
        bit1, bit0 = (m // 2) % 2, m % 2
        mine = own.at[stream, c]
        src, slot, off, cond = (
            (mine, 2, 4, m + 4 < n),
            (mine, 1, 2, bit1 == 0),
            (mine, 0, 1, bit0 == 0),
            (slots.at[stream, 2, c], 3, 4, jnp.logical_and(m >= 4, m + 4 < n)),
            (slots.at[stream, 2, c], 1, -2, jnp.logical_and(m >= 4, bit1 == 1)),
            (slots.at[stream, 1, c], 0, -1, jnp.logical_and(m >= 2, bit0 == 1)),
        )[kind]
        copy = pltpu.make_async_remote_copy(
            src_ref=src, dst_ref=slots.at[stream, slot, c],
            send_sem=send_sem.at[stream, kind, c], recv_sem=recv_sem.at[stream, slot, c],
            device_id={"frame": i + sign * off}, device_id_type=pl.DeviceIdType.MESH)
        return copy, cond

    def send(stream, kind, c):
        copy, cond = hop(stream, kind, c)

        @pl.when(cond)
        def _():
            copy.start()

    def arrive(stream, slot, c):
        m, sign = place(stream)

        @pl.when(m >= 2**slot)
        def _():
            pltpu.make_async_remote_copy(
                src_ref=own.at[stream, c], dst_ref=slots.at[stream, slot, c],
                send_sem=send_sem.at[stream, 0, c], recv_sem=recv_sem.at[stream, slot, c],
                device_id={"frame": i - sign * 2**slot},
                device_id_type=pl.DeviceIdType.MESH).wait_recv()

    def message(j, c):
        return pltpu.make_async_remote_copy(
            src_ref=msg_out.at[c, j + 1], dst_ref=msg_in.at[c, j],
            send_sem=msg_send.at[j, c], recv_sem=msg_recv.at[j, c],
            device_id={"frame": i - 2**j}, device_id_type=pl.DeviceIdType.MESH)

    for c in range(chunks):
        for stream in range(2):
            for part in range(2):
                load(stream, part, c).start()
    w_copies = [pltpu.make_async_copy(w, weights.at[x], w_sem.at[x])
                for x, w in enumerate((wq_ref, wk_ref, wv_ref))]
    for copy in w_copies:
        copy.start()

    barrier = pltpu.get_barrier_semaphore()
    peers = jnp.int32(0)
    for j in range(NDIL):
        for off in (2**j, -(2**j)):
            there = jnp.logical_and(i + off >= 0, i + off < n)
            peers = peers + there.astype(jnp.int32)

            @pl.when(there)
            def _():
                pl.semaphore_signal(barrier, inc=1, device_id={"frame": i + off},
                                    device_id_type=pl.DeviceIdType.MESH)
    pl.semaphore_wait(barrier, peers)

    def direct(c):
        for stream in range(2):
            for part in range(2):
                load(stream, part, c).wait()
        for kind in range(3):
            for stream in range(2):
                send(stream, kind, c)

    for c in range(min(AHEAD, chunks)):
        direct(c)

    feature = lax.broadcasted_iota(jnp.int32, (width, LANES), 0) // head
    lane = lax.broadcasted_iota(jnp.int32, (width, LANES), 1) % HEADS
    gather[...] = jnp.where(feature == lane, 1.0, 0.0).astype(bf16)
    lane = lax.broadcasted_iota(jnp.int32, (LANES, width), 0)
    feature = lax.broadcasted_iota(jnp.int32, (LANES, width), 1) // head
    for x in range(4):
        hit = jnp.logical_and(lane % HEADS == feature, lane // (2 * HEADS) == x)
        spread[x] = jnp.where(hit, 1.0, 0.0).astype(bf16)

    for stream in range(2):
        m, _ = place(stream)
        for j in range(NDIL):
            @pl.when(m < 2**j)
            def _():
                for c in range(chunks):
                    for part in range(2):
                        slots[stream, j, c, part] = jnp.zeros((rows, width), bf16)
                    if stream == 1:
                        msg_in[c, j] = jnp.zeros((half, LANES), bf16)
    for copy in w_copies:
        copy.wait()

    def relay_far(c):
        for stream in range(2):
            arrive(stream, 2, c)
            send(stream, 4, c)
            send(stream, 3, c)

    def relay_near(c):
        for stream in range(2):
            arrive(stream, 1, c)
            send(stream, 5, c)

    def attend(c):
        for slot in (0, 3):
            arrive(0, slot, c)
        for part in range(2):
            left = own[1, c, part].astype(f32)
            for j in range(NDIL + 1):
                right = own[0, c, part] if j == 0 else slots[0, j - 1, c, part]
                product = left * right.astype(f32)
                high = product.astype(bf16)
                low = (product - high.astype(f32)).astype(bf16)
                at = (part * (NDIL + 1) + j) * 2 * rows
                prods[at:at + rows] = high
                prods[at + rows:at + 2 * rows] = low
        sums = dot_nn(prods[...], gather[...])

        def reduced(part, j):
            at = (part * (NDIL + 1) + j) * 2 * rows
            return sums[at:at + rows] + sums[at + rows:at + 2 * rows]

        live = [None] + [(links_ref[0, j] > 0).astype(f32) for j in range(NDIL)]
        scores = [reduced(0, j) * scale for j in range(NDIL + 1)]
        scores = [s if j == 0 else jnp.where(live[j] > 0, s, -1e30)
                  for j, s in enumerate(scores)]
        highest = functools.reduce(jnp.maximum, scores)
        raw = [jnp.exp(s - highest) for s in scores]
        raw = [r if j == 0 else r * live[j] for j, r in enumerate(raw)]
        total = functools.reduce(jnp.add, raw)
        probability = [r / total for r in raw]
        grad_prob = [reduced(1, j) for j in range(NDIL + 1)]
        inner = functools.reduce(
            jnp.add, [p * g for p, g in zip(probability, grad_prob)])
        lanes = lax.broadcasted_iota(jnp.int32, (rows, LANES), 1)
        group = (lanes // HEADS) % 4
        lower = lanes[:half] < LANES // 2
        for j in range(NDIL + 1):
            prob = probability[j]
            grad_score = prob * (grad_prob[j] - inner) * scale
            value = jnp.where(group < 2, grad_score, prob)
            high = value.astype(bf16).astype(f32)
            value = jnp.where(group % 2 == 0, high, value - high)
            msg_out[c, j] = jnp.where(lower, value[:half], value[half:]).astype(bf16)
        for j in range(NDIL):
            @pl.when(i >= 2**j)
            def _():
                message(j, c).start()

    def finish(c):
        packed = msg_out[c].reshape((NDIL + 1) * half, LANES)
        halves = []
        for h in range(2):
            at = slice(h * half, (h + 1) * half)
            score = dot_nn(packed, spread[2 * h])
            total = score[:half] * own[0, c, 0, at].astype(f32)
            for j in range(NDIL):
                total += (score[(j + 1) * half:(j + 2) * half]
                          * slots[0, j, c, 0, at].astype(f32))
            halves.append(total.astype(bf16))
        result = dot_nt(jnp.concatenate(halves, axis=0), weights[0])

        for slot in (0, 3):
            arrive(1, slot, c)
        for j in range(NDIL):
            @pl.when(i + 2**j < n)
            def _():
                message(j, c).wait_recv()
        packed = jnp.concatenate(
            [msg_out[c, 0], msg_in[c].reshape(NDIL * half, LANES)], axis=0)
        for part in range(2):
            halves = []
            for h in range(2):
                at = slice(h * half, (h + 1) * half)
                factor = dot_nn(packed, spread[2 * h + part])
                total = factor[:half] * own[1, c, part, at].astype(f32)
                for j in range(NDIL):
                    total += (factor[(j + 1) * half:(j + 2) * half]
                              * slots[1, j, c, part, at].astype(f32))
                halves.append(total.astype(bf16))
            result += dot_nt(jnp.concatenate(halves, axis=0), weights[1 + part])
        out_ref[0, pl.ds(pl.multiple_of(c * rows, rows), rows), :] = result.astype(bf16)

    def step(s, carry):
        @pl.when(s < chunks)
        def _():
            relay_far(s)

        @pl.when(s + AHEAD < chunks)
        def _():
            direct(s + AHEAD)

        @pl.when(jnp.logical_and(s >= 1, s < chunks + 1))
        def _():
            relay_near(s - 1)

        @pl.when(jnp.logical_and(s >= 2, s < chunks + 2))
        def _():
            attend(s - 2)

        @pl.when(s >= 3)
        def _():
            finish(s - 3)
        return carry

    lax.fori_loop(0, chunks + 3, step, 0)

    def drain(c, carry):
        for stream in range(2):
            for kind in range(6):
                copy, cond = hop(stream, kind, c)

                @pl.when(cond)
                def _():
                    copy.wait_send()
        for j in range(NDIL):
            @pl.when(i >= 2**j)
            def _():
                message(j, c).wait_send()
        return carry

    lax.fori_loop(0, chunks, drain, 0)


def per_device(queries, keys, values, grad_out, links, w_query, w_key, w_value):
    frames, patches, width = queries.shape
    n = lax.axis_size("frame")
    rows = 64
    chunks = patches // rows
    half = rows // 2
    hbm = pl.BlockSpec(memory_space=pl.ANY)
    bf16 = jnp.bfloat16
    dma = pltpu.SemaphoreType.DMA
    return pl.pallas_call(
        functools.partial(kernel, n, chunks, rows),
        out_shape=jax.ShapeDtypeStruct((frames, patches, width), bf16),
        in_specs=[pl.BlockSpec(memory_space=pltpu.SMEM)] + [hbm] * 7,
        out_specs=pl.BlockSpec(memory_space=pltpu.VMEM),
        scratch_shapes=[
            pltpu.VMEM((2, chunks, 2, rows, width), bf16),
            pltpu.VMEM((2, NDIL, chunks, 2, rows, width), bf16),
            pltpu.VMEM((chunks, NDIL + 1, half, LANES), bf16),
            pltpu.VMEM((chunks, NDIL, half, LANES), bf16),
            pltpu.VMEM(((NDIL + 1) * 4 * rows, width), bf16),
            pltpu.VMEM((width, LANES), bf16),
            pltpu.VMEM((4, LANES, width), bf16),
            pltpu.VMEM((3, width, width), bf16),
            dma((2, 2, chunks)),
            dma((3,)),
            dma((2, 6, chunks)),
            dma((2, NDIL, chunks)),
            dma((NDIL, chunks)),
            dma((NDIL, chunks)),
        ],
        compiler_params=pltpu.CompilerParams(
            collective_id=0, has_side_effects=True, vmem_limit_bytes=60 * 1024 * 1024),
    )(links, queries, keys, values, grad_out, w_query, w_key, w_value)


def solution(mesh):
    placed = (
        P(("dom", "frame"), None, None),
        P(("dom", "frame"), None, None),
        P(("dom", "frame"), None, None),
        P(("dom", "frame"), None, None),
        P(("dom", "frame"), None),
        P(),
        P(),
        P(),
    )
    return jax.shard_map(
        per_device,
        mesh=mesh,
        in_specs=placed,
        out_specs=P(("dom", "frame"), None, None),
        check_vma=False,
    )
```

time: 283 us -> 117 us (0.41)
  waiting for transfers between devices: 178 us -> 0 us
  Pallas kernels: 0 us -> 115 us
  local copies, waits for them, and re-layouts: 41.9 us -> 2.26 us
  starting transfers between devices: 27.3 us -> 0 us
  other arithmetic: 26.3 us -> 0 us
  matrix products: 4.93 us -> 0 us
  between operations: 3.09 us -> 0.01 us
    ppermute x12 -> x0, waiting for transfers between devices: 178 us -> none  [from_behind(): return lax.ppermute(block, axis, route)]
    pallas_call x0 -> x1, Pallas kernels: none -> 115 us  [per_device(): pl.pallas_call(functools.partial(kernel, n, chunks, rows), out_shape=jax....]
    ppermute x12 -> x0, starting transfers between devices: 27.3 us -> none  [from_behind(): return lax.ppermute(block, axis, route)]
    convert_element_type x6 -> x0, other arithmetic: 16.1 us -> none  [the longest x4 7.68 us: spread_heads(): return a.astype(jnp.float32).reshape(frames, patches, HEADS, head_size)]
    mul x18 -> x0, local copies, waits for them, and re-layouts: 13.9 us -> none  [the longest x8 6.35 us: per_device(): came_weights[0][..., None] * spread_heads(came_inputs[0])]
    reshape x4 -> x0, local copies, waits for them, and re-layouts: 7.8 us -> none  [per_device(): jnp.stack([grad_score[j + 1], probability[j + 1]])]
    slice x5 -> x0, local copies, waits for them, and re-layouts: 7.48 us -> none  [the longest x4 6.82 us: per_device(): came_weights[0][..., None] * spread_heads(came_inputs[0])]
    unnamed x38 -> x1, local copies, waits for them, and re-layouts: 8.54 us -> 2.26 us
  transfers between devices with their start and end apart: 12 -> 0, of which waited for: 6 -> 0; matrix products, arithmetic and copies ran while one was open for 19% -> 0% of each run, Pallas kernels for 0% -> 0%
where the time goes in v1:
time: 117 us
  Pallas kernels  115 us (98%)
  local copies, waits for them, and re-layouts  2.26 us (2%)
    pallas_call x1, Pallas kernels, per_device(): pl.pallas_call(functools.partial(kernel, n, chunks, rows), out_shape=jax....  115 us

profile of v1, /device:TPU:0, one launch (start us, length us, event | category | flops | bytes accessed | tf_op | source)
XLA Modules:
  0.0 117.1 jit_solution(12327164103332769110)
XLA Ops:
  0.0 114.8 %shard_map.82 = bf16[1,512,1024]{2,1,0:T(8,128)(2,1)} custom-call(s32[1,4]{1,0:T(1,128)} %links_ref.1, bf16[1,512,1024]{2,1,0:T(8,128)(2,1)} %q_ref.1, bf16[1,512,1024]{2,1,0:T(8,128)(2,1)} %k_ref.1, bf16[1,512,1024]{2,1,0:T(8,128)(2,1)} %v_ref.1, bf16[1,512,1024]{2,1,0:T(8,128)(2,1)} %g_ref.1, bf16[1024,1024]{1,0:T(8,128)(2,1)} %wq_ref.1, ...), custom_call_target="tpu_custom_call" | custom-call | tf_op jit(solution)/shard_map/pallas_call | solution.py:285
  114.8 2.3 %copy.10 = bf16[1,512,1024]{2,1,0:T(8,128)(2,1)} copy(bf16[1,512,1024]{2,1,0:T(8,128)(2,1)} %shard_map.82) | data formatting | bytes 2097152

commit v2 on v1

v2 whole, which is shorter than its diff:
```python
import functools

import jax
import jax.numpy as jnp
from jax import lax
from jax.experimental import pallas as pl
from jax.experimental.pallas import tpu as pltpu
from jax.sharding import PartitionSpec as P

HEADS = 16
NDIL = 4
LANES = 128
AHEAD = 3
LAGS = (0, 1, 2, 3, 4, 5)


def dot_nt(left, right):
    return lax.dot_general(
        left, right, (((1,), (1,)), ((), ())), preferred_element_type=jnp.float32
    )


def dot_nn(left, right):
    return lax.dot_general(
        left, right, (((1,), (0,)), ((), ())), preferred_element_type=jnp.float32
    )


def kernel(n, chunks, rows, links_ref, q_ref, k_ref, v_ref, g_ref, wq_ref, wk_ref, wv_ref,
           out_ref, ahead, back, local, ahead_in, back_in, part_out, part_in,
           prob_out, prob_in, dot_out, dot_in, kept, kept_mid, kept_near, base,
           prods, gather, spread, fold, weights,
           own_sem, w_sem, send_sem, recv_sem, prob_send, prob_recv, dot_send, dot_recv,
           part_send, part_recv):
    width = q_ref.shape[-1]
    head = width // HEADS
    scale = head ** (-0.5)
    half = rows // 2
    count = NDIL + 1
    i = lax.axis_index("frame")
    f32, bf16 = jnp.float32, jnp.bfloat16

    own = (ahead, back)
    slots = (ahead_in, back_in)

    def place(stream):
        return (i, 1) if stream == 0 else (n - 1 - i, -1)

    def loads(c):
        plan = ((k_ref, 0, ahead, 0), (k_ref, 1, ahead, 1), (v_ref, 1, ahead, 2),
                (q_ref, 0, back, 0), (g_ref, 0, back, 1),
                (v_ref, 0, local, 0), (q_ref, 1, local, 1), (g_ref, 1, local, 2))
        return [pltpu.make_async_copy(
            src.at[0, pl.ds(pl.multiple_of((2 * c + side) * rows, rows), rows), :],
            dst.at[c, part], own_sem.at[x, c])
            for x, (src, side, dst, part) in enumerate(plan)]

    def hop(stream, kind, c):
        m, sign = place(stream)
        bit1, bit0 = (m // 2) % 2, m % 2
        mine, into = own[stream].at[c], slots[stream]
        src, slot, off, cond = (
            (mine, 2, 4, m + 4 < n),
            (mine, 1, 2, bit1 == 0),
            (mine, 0, 1, bit0 == 0),
            (into.at[2, c], 3, 4, jnp.logical_and(m >= 4, m + 4 < n)),
            (into.at[2, c], 1, -2, jnp.logical_and(m >= 4, bit1 == 1)),
            (into.at[1, c], 0, -1, jnp.logical_and(m >= 2, bit0 == 1)),
        )[kind]
        copy = pltpu.make_async_remote_copy(
            src_ref=src, dst_ref=into.at[slot, c],
            send_sem=send_sem.at[stream, kind, c], recv_sem=recv_sem.at[stream, slot, c],
            device_id={"frame": i + sign * off}, device_id_type=pl.DeviceIdType.MESH)
        return copy, cond

    def send(stream, kind, c):
        copy, cond = hop(stream, kind, c)

        @pl.when(cond)
        def _():
            copy.start()

    def arrive(stream, slot, c):
        m, sign = place(stream)

        @pl.when(m >= 2**slot)
        def _():
            pltpu.make_async_remote_copy(
                src_ref=own[stream].at[c], dst_ref=slots[stream].at[slot, c],
                send_sem=send_sem.at[stream, 0, c], recv_sem=recv_sem.at[stream, slot, c],
                device_id={"frame": i - sign * 2**slot},
                device_id_type=pl.DeviceIdType.MESH).wait_recv()

    def returns(slot):
        bit1, bit0 = (i // 2) % 2, i % 2
        if slot == 2:
            return [(0, -4, i >= 4)]
        if slot == 3:
            return [(3, -4, i >= 8)]
        if slot == 1:
            return [(1, -2, jnp.logical_and(i >= 2, bit1 == 1)),
                    (4, 2, jnp.logical_and(i >= 2, bit1 == 0))]
        return [(2, -1, bit0 == 1), (5, 1, jnp.logical_and(i >= 1, bit0 == 0))]

    def back_copy(slot, kind, off, c):
        return pltpu.make_async_remote_copy(
            src_ref=part_out.at[slot, c], dst_ref=part_in.at[kind, c],
            send_sem=part_send.at[slot, c], recv_sem=part_recv.at[kind, c],
            device_id={"frame": i + off}, device_id_type=pl.DeviceIdType.MESH)

    def give_back(slot, c):
        for kind, off, cond in returns(slot):
            @pl.when(cond)
            def _():
                back_copy(slot, kind, off, c).start()

    def add_back(kind, c, ref):
        cond = hop(0, kind, c)[1]
        off = (4, 2, 1, 4, -2, -1)[kind]

        @pl.when(cond)
        def _():
            pltpu.make_async_remote_copy(
                src_ref=part_out.at[0, c], dst_ref=part_in.at[kind, c],
                send_sem=part_send.at[0, c], recv_sem=part_recv.at[kind, c],
                device_id={"frame": i + off},
                device_id_type=pl.DeviceIdType.MESH).wait_recv()
            ref[c] += part_in[kind, c].astype(f32)

    def prob_copy(j, c):
        return pltpu.make_async_remote_copy(
            src_ref=prob_out.at[c, j + 1], dst_ref=prob_in.at[c, j],
            send_sem=prob_send.at[j, c], recv_sem=prob_recv.at[j, c],
            device_id={"frame": i - 2**j}, device_id_type=pl.DeviceIdType.MESH)

    def dot_copy(j, c):
        return pltpu.make_async_remote_copy(
            src_ref=dot_out.at[c, j], dst_ref=dot_in.at[c, j],
            send_sem=dot_send.at[j, c], recv_sem=dot_recv.at[j, c],
            device_id={"frame": i + 2**j}, device_id_type=pl.DeviceIdType.MESH)

    for c in range(chunks):
        for copy in loads(c):
            copy.start()
    w_copies = [pltpu.make_async_copy(w, weights.at[x], w_sem.at[x])
                for x, w in enumerate((wq_ref, wk_ref, wv_ref))]
    for copy in w_copies:
        copy.start()

    barrier = pltpu.get_barrier_semaphore()
    peers = jnp.int32(0)
    for j in range(NDIL):
        for off in (2**j, -(2**j)):
            there = jnp.logical_and(i + off >= 0, i + off < n)
            peers = peers + there.astype(jnp.int32)

            @pl.when(there)
            def _():
                pl.semaphore_signal(barrier, inc=1, device_id={"frame": i + off},
                                    device_id_type=pl.DeviceIdType.MESH)
    pl.semaphore_wait(barrier, peers)

    def direct(c):
        for copy in loads(c):
            copy.wait()
        for kind in range(3):
            for stream in range(2):
                send(stream, kind, c)

    for c in range(min(AHEAD, chunks)):
        direct(c)

    feature = lax.broadcasted_iota(jnp.int32, (width, LANES), 0) // head
    lane = lax.broadcasted_iota(jnp.int32, (width, LANES), 1) % HEADS
    gather[...] = jnp.where(feature == lane, 1.0, 0.0).astype(bf16)
    lane = lax.broadcasted_iota(jnp.int32, (LANES, width), 0)
    feature = lax.broadcasted_iota(jnp.int32, (LANES, width), 1) // head
    for x in range(4):
        hit = jnp.logical_and(lane % HEADS == feature, lane // (2 * HEADS) == x)
        spread[x] = jnp.where(hit, 1.0, 0.0).astype(bf16)
    lane = lax.broadcasted_iota(jnp.int32, (LANES, LANES), 0)
    feature = lax.broadcasted_iota(jnp.int32, (LANES, LANES), 1)
    for x in range(2):
        hit = jnp.logical_and(lane % HEADS == feature % HEADS, lane // (2 * HEADS) == 2 * x)
        fold[x] = jnp.where(hit, 1.0, 0.0).astype(bf16)

    for j in range(NDIL):
        @pl.when(i < 2**j)
        def _():
            for c in range(chunks):
                for part in range(3):
                    ahead_in[j, c, part] = jnp.zeros((rows, width), bf16)
                dot_in[c, j] = jnp.zeros((half, LANES), bf16)

        @pl.when(i + 2**j >= n)
        def _():
            for c in range(chunks):
                for part in range(2):
                    back_in[j, c, part] = jnp.zeros((rows, width), bf16)
                prob_in[c, j] = jnp.zeros((half, LANES), bf16)
    for copy in w_copies:
        copy.wait()

    lanes = lax.broadcasted_iota(jnp.int32, (rows, LANES), 1)
    group = (lanes // HEADS) % 4
    lower = lanes[:half] < LANES // 2

    def pack(value):
        return jnp.where(lower, value[:half], value[half:]).astype(bf16)

    def softmax_back(scores, grad_prob):
        live = [None] + [(links_ref[0, j] > 0).astype(f32) for j in range(NDIL)]
        scores = [s if j == 0 else jnp.where(live[j] > 0, s, -1e30)
                  for j, s in enumerate(scores)]
        highest = functools.reduce(jnp.maximum, scores)
        raw = [jnp.exp(s - highest) for s in scores]
        raw = [r if j == 0 else r * live[j] for j, r in enumerate(raw)]
        total = functools.reduce(jnp.add, raw)
        probability = [r / total for r in raw]
        inner = functools.reduce(
            jnp.add, [p * g for p, g in zip(probability, grad_prob)])
        values = []
        for prob, grad in zip(probability, grad_prob):
            grad_score = prob * (grad - inner) * scale
            value = jnp.where(group < 2, grad_score, prob)
            high = value.astype(bf16).astype(f32)
            values.append(jnp.where(group % 2 == 0, high, value - high))
        return values

    def relay_far(c):
        for stream in range(2):
            arrive(stream, 2, c)
            send(stream, 4, c)
            send(stream, 3, c)

    def relay_near(c):
        for stream in range(2):
            arrive(stream, 1, c)
            send(stream, 5, c)

    def query_grad(values, part, c):
        stack = jnp.concatenate([v.astype(bf16) for v in values], axis=0)
        factor = dot_nn(stack, spread[0])
        total = factor[:rows] * ahead[c, part].astype(f32)
        for j in range(NDIL):
            total += (factor[(j + 1) * rows:(j + 2) * rows]
                      * ahead_in[j, c, part].astype(f32))
        return total.astype(bf16), stack, factor

    def attend(c):
        for slot in (0, 3):
            for stream in range(2):
                arrive(stream, slot, c)
        pairs = (
            [(back[c, 0], ahead[c, 0])]
            + [(back[c, 0], ahead_in[j, c, 0]) for j in range(NDIL)]
            + [(back[c, 1], local[c, 0])]
            + [(back_in[j, c, 1], local[c, 0]) for j in range(NDIL)]
            + [(local[c, 1], ahead[c, 1])]
            + [(local[c, 1], ahead_in[j, c, 1]) for j in range(NDIL)]
            + [(local[c, 2], ahead[c, 2])]
            + [(local[c, 2], ahead_in[j, c, 2]) for j in range(NDIL)])
        for x, (left, right) in enumerate(pairs):
            product = left.astype(f32) * right.astype(f32)
            high = product.astype(bf16)
            low = (product - high.astype(f32)).astype(bf16)
            prods[2 * x * rows:(2 * x + 1) * rows] = high
            prods[(2 * x + 1) * rows:(2 * x + 2) * rows] = low
        sums = dot_nn(prods[...], gather[...])

        def reduced(x):
            return (sums[2 * x * rows:(2 * x + 1) * rows]
                    + sums[(2 * x + 1) * rows:(2 * x + 2) * rows])

        for j in range(NDIL):
            value = reduced(count + 1 + j)
            high = value.astype(bf16).astype(f32)
            dot_out[c, j] = pack(jnp.where(group % 2 == 0, high, value - high))

            @pl.when(i + 2**j < n)
            def _():
                dot_copy(j, c).start()
        for x in range(count + 1):
            kept[c, x] = reduced(x)

        values = softmax_back(
            [reduced(2 * count + j) * scale for j in range(count)],
            [reduced(3 * count + j) for j in range(count)])
        query_part, stack, key_factor = query_grad(values, 1, c)
        value_factor = dot_nn(stack, spread[1])
        q_rows, g_rows = local[c, 1].astype(f32), local[c, 2].astype(f32)
        key_parts = jnp.concatenate(
            [(key_factor[j * rows:(j + 1) * rows] * q_rows).astype(bf16)
             for j in range(count)], axis=0)
        value_parts = jnp.concatenate(
            [(value_factor[j * rows:(j + 1) * rows] * g_rows).astype(bf16)
             for j in range(count)], axis=0)
        projected = dot_nt(key_parts, weights[1]) + dot_nt(value_parts, weights[2])

        def at(slot):
            return projected[(slot + 1) * rows:(slot + 2) * rows]

        for slot in (0, 3):
            part_out[slot, c] = at(slot).astype(bf16)
            give_back(slot, c)
        kept_near[c] = at(1)
        kept_mid[c] = at(2)
        base[c] = projected[:rows] + dot_nt(query_part, weights[0])

    def soften(c):
        for j in range(NDIL):
            @pl.when(i >= 2**j)
            def _():
                dot_copy(j, c).wait_recv()
        packed = dot_in[c].reshape(NDIL * half, LANES)
        folded = [dot_nn(packed, fold[x]) for x in range(2)]
        grad_prob = [kept[c, count]] + [
            jnp.concatenate([f[j * half:(j + 1) * half] for f in folded], axis=0)
            for j in range(NDIL)]
        values = softmax_back([kept[c, j] * scale for j in range(count)], grad_prob)
        for j in range(count):
            prob_out[c, j] = pack(values[j])
        for j in range(NDIL):
            @pl.when(i >= 2**j)
            def _():
                prob_copy(j, c).start()
        add_back(5, c, kept_near)
        part_out[1, c] = kept_near[c].astype(bf16)
        give_back(1, c)

    def finish(c):
        add_back(3, c, kept_mid)
        add_back(4, c, kept_mid)
        part_out[2, c] = kept_mid[c].astype(bf16)
        give_back(2, c)

        packed = prob_out[c].reshape(count * half, LANES)
        halves = []
        for h in range(2):
            at = slice(h * half, (h + 1) * half)
            score = dot_nn(packed, spread[2 * h])
            total = score[:half] * ahead[c, 0, at].astype(f32)
            for j in range(NDIL):
                total += (score[(j + 1) * half:(j + 2) * half]
                          * ahead_in[j, c, 0, at].astype(f32))
            halves.append(total.astype(bf16))
        result = dot_nt(jnp.concatenate(halves, axis=0), weights[0])
        for j in range(NDIL):
            @pl.when(i + 2**j < n)
            def _():
                prob_copy(j, c).wait_recv()
        packed = jnp.concatenate(
            [prob_out[c, 0], prob_in[c].reshape(NDIL * half, LANES)], axis=0)
        for part in range(2):
            halves = []
            for h in range(2):
                at = slice(h * half, (h + 1) * half)
                factor = dot_nn(packed, spread[2 * h + part])
                total = factor[:half] * back[c, part, at].astype(f32)
                for j in range(NDIL):
                    total += (factor[(j + 1) * half:(j + 2) * half]
                              * back_in[j, c, part, at].astype(f32))
                halves.append(total.astype(bf16))
            result += dot_nt(jnp.concatenate(halves, axis=0), weights[1 + part])
        out_ref[0, pl.ds(pl.multiple_of(2 * c * rows, rows), rows), :] = result.astype(bf16)

    def collect(c):
        for kind in (2, 1, 0):
            add_back(kind, c, base)
        out_ref[0, pl.ds(pl.multiple_of((2 * c + 1) * rows, rows), rows), :] = (
            base[c].astype(bf16))

    def step(s, carry):
        def stage(lag, run):
            @pl.when(jnp.logical_and(s >= lag, s < chunks + lag))
            def _():
                run(s - lag)

        stage(LAGS[0], relay_far)
        stage(LAGS[1], relay_near)

        @pl.when(s + AHEAD < chunks)
        def _():
            direct(s + AHEAD)

        stage(LAGS[2], attend)
        stage(LAGS[3], soften)
        stage(LAGS[4], finish)
        stage(LAGS[5], collect)
        return carry

    lax.fori_loop(0, chunks + LAGS[5], step, 0)

    def drain(c, carry):
        for stream in range(2):
            for kind in range(6):
                copy, cond = hop(stream, kind, c)

                @pl.when(cond)
                def _():
                    copy.wait_send()
        for j in range(NDIL):
            for kind, off, cond in returns(j):
                @pl.when(cond)
                def _():
                    back_copy(j, kind, off, c).wait_send()

            @pl.when(i >= 2**j)
            def _():
                prob_copy(j, c).wait_send()

            @pl.when(i + 2**j < n)
            def _():
                dot_copy(j, c).wait_send()
        return carry

    lax.fori_loop(0, chunks, drain, 0)


def per_device(queries, keys, values, grad_out, links, w_query, w_key, w_value):
    frames, patches, width = queries.shape
    n = lax.axis_size("frame")
    rows = 32
    chunks = patches // (2 * rows)
    half = rows // 2
    hbm = pl.BlockSpec(memory_space=pl.ANY)
    f32, bf16 = jnp.float32, jnp.bfloat16
    dma = pltpu.SemaphoreType.DMA
    return pl.pallas_call(
        functools.partial(kernel, n, chunks, rows),
        out_shape=jax.ShapeDtypeStruct((frames, patches, width), bf16),
        in_specs=[pl.BlockSpec(memory_space=pltpu.SMEM)] + [hbm] * 7,
        out_specs=pl.BlockSpec(memory_space=pltpu.VMEM),
        scratch_shapes=[
            pltpu.VMEM((chunks, 3, rows, width), bf16),
            pltpu.VMEM((chunks, 2, rows, width), bf16),
            pltpu.VMEM((chunks, 3, rows, width), bf16),
            pltpu.VMEM((NDIL, chunks, 3, rows, width), bf16),
            pltpu.VMEM((NDIL, chunks, 2, rows, width), bf16),
            pltpu.VMEM((NDIL, chunks, rows, width), bf16),
            pltpu.VMEM((6, chunks, rows, width), bf16),
            pltpu.VMEM((chunks, NDIL + 1, half, LANES), bf16),
            pltpu.VMEM((chunks, NDIL, half, LANES), bf16),
            pltpu.VMEM((chunks, NDIL, half, LANES), bf16),
            pltpu.VMEM((chunks, NDIL, half, LANES), bf16),
            pltpu.VMEM((chunks, NDIL + 2, rows, LANES), f32),
            pltpu.VMEM((chunks, rows, width), f32),
            pltpu.VMEM((chunks, rows, width), f32),
            pltpu.VMEM((chunks, rows, width), f32),
            pltpu.VMEM((8 * (NDIL + 1) * rows, width), bf16),
            pltpu.VMEM((width, LANES), bf16),
            pltpu.VMEM((4, LANES, width), bf16),
            pltpu.VMEM((2, LANES, LANES), bf16),
            pltpu.VMEM((3, width, width), bf16),
            dma((8, chunks)),
            dma((3,)),
            dma((2, 6, chunks)),
            dma((2, NDIL, chunks)),
            dma((NDIL, chunks)),
            dma((NDIL, chunks)),
            dma((NDIL, chunks)),
            dma((NDIL, chunks)),
            dma((NDIL, chunks)),
            dma((6, chunks)),
        ],
        compiler_params=pltpu.CompilerParams(
            collective_id=0, has_side_effects=True, vmem_limit_bytes=60 * 1024 * 1024),
    )(links, queries, keys, values, grad_out, w_query, w_key, w_value)


def solution(mesh):
    placed = (
        P(("dom", "frame"), None, None),
        P(("dom", "frame"), None, None),
        P(("dom", "frame"), None, None),
        P(("dom", "frame"), None, None),
        P(("dom", "frame"), None),
        P(),
        P(),
        P(),
    )
    return jax.shard_map(
        per_device,
        mesh=mesh,
        in_specs=placed,
        out_specs=P(("dom", "frame"), None, None),
        check_vma=False,
    )
```

time: 117 us -> 111 us (0.949)
  Pallas kernels: 115 us -> 109 us
    pallas_call x1, Pallas kernels: 115 us -> 109 us  [per_device(): pl.pallas_call(functools.partial(kernel, n, chunks, rows), out_shape=jax....]
where the time goes in v2:
time: 111 us
  Pallas kernels  109 us (98%)
  local copies, waits for them, and re-layouts  2.26 us (2%)
    pallas_call x1, Pallas kernels, per_device(): pl.pallas_call(functools.partial(kernel, n, chunks, rows), out_shape=jax....  109 us
    unnamed x1, local copies, waits for them, and re-layouts  2.26 us

profile of v2, /device:TPU:0, one launch (start us, length us, event | category | flops | bytes accessed | tf_op | source)
XLA Modules:
  0.0 111.0 jit_solution(3873360461951081718)
XLA Ops:
  0.0 108.8 %shard_map.82 = bf16[1,512,1024]{2,1,0:T(8,128)(2,1)} custom-call(s32[1,4]{1,0:T(1,128)} %links_ref.1, bf16[1,512,1024]{2,1,0:T(8,128)(2,1)} %q_ref.1, bf16[1,512,1024]{2,1,0:T(8,128)(2,1)} %k_ref.1, bf16[1,512,1024]{2,1,0:T(8,128)(2,1)} %v_ref.1, bf16[1,512,1024]{2,1,0:T(8,128)(2,1)} %g_ref.1, bf16[1024,1024]{1,0:T(8,128)(2,1)} %wq_ref.1, ...), custom_call_target="tpu_custom_call" | custom-call | tf_op jit(solution)/shard_map/pallas_call | solution.py:429
  108.8 2.3 %copy.10 = bf16[1,512,1024]{2,1,0:T(8,128)(2,1)} copy(bf16[1,512,1024]{2,1,0:T(8,128)(2,1)} %shard_map.82) | data formatting | bytes 2097152

commit v3 on v2

--- a/solution.py
+++ b/solution.py
@@ -11,13 +11,7 @@
 NDIL = 4
 LANES = 128
 AHEAD = 3
-LAGS = (0, 1, 2, 3, 4, 5)
-
-
-def dot_nt(left, right):
-    return lax.dot_general(
-        left, right, (((1,), (1,)), ((), ())), preferred_element_type=jnp.float32
-    )
+LAGS = (0, 1, 2, 4, 6, 8)
 
 
 def dot_nn(left, right):
@@ -28,8 +22,8 @@
 
 def kernel(n, chunks, rows, links_ref, q_ref, k_ref, v_ref, g_ref, wq_ref, wk_ref, wv_ref,
            out_ref, ahead, back, local, ahead_in, back_in, part_out, part_in,
-           prob_out, prob_in, dot_out, dot_in, kept, kept_mid, kept_near, base,
-           prods, gather, spread, fold, weights,
+           prob_out, prob_in, dot_out, dot_in, kept, kept_mid, kept_near, base, own_part,
+           prods, gather, spread, fold, stored, weights,
            own_sem, w_sem, send_sem, recv_sem, prob_send, prob_recv, dot_send, dot_recv,
            part_send, part_recv):
     width = q_ref.shape[-1]
@@ -142,7 +136,7 @@
     for c in range(chunks):
         for copy in loads(c):
             copy.start()
-    w_copies = [pltpu.make_async_copy(w, weights.at[x], w_sem.at[x])
+    w_copies = [pltpu.make_async_copy(w, stored.at[x], w_sem.at[x])
                 for x, w in enumerate((wq_ref, wk_ref, wv_ref))]
     for copy in w_copies:
         copy.start()
@@ -198,9 +192,6 @@
                 for part in range(2):
                     back_in[j, c, part] = jnp.zeros((rows, width), bf16)
                 prob_in[c, j] = jnp.zeros((half, LANES), bf16)
-    for copy in w_copies:
-        copy.wait()
-
     lanes = lax.broadcasted_iota(jnp.int32, (rows, LANES), 1)
     group = (lanes // HEADS) % 4
     lower = lanes[:half] < LANES // 2
@@ -295,17 +286,20 @@
         value_parts = jnp.concatenate(
             [(value_factor[j * rows:(j + 1) * rows] * g_rows).astype(bf16)
              for j in range(count)], axis=0)
-        projected = dot_nt(key_parts, weights[1]) + dot_nt(value_parts, weights[2])
+        projected = (dot_nn(key_parts[rows:], weights[1])
+                     + dot_nn(value_parts[rows:], weights[2]))
 
         def at(slot):
-            return projected[(slot + 1) * rows:(slot + 2) * rows]
+            return projected[slot * rows:(slot + 1) * rows]
 
         for slot in (0, 3):
             part_out[slot, c] = at(slot).astype(bf16)
             give_back(slot, c)
         kept_near[c] = at(1)
         kept_mid[c] = at(2)
-        base[c] = projected[:rows] + dot_nt(query_part, weights[0])
+        own_part[c, 0] = query_part
+        own_part[c, 1] = key_parts[:rows]
+        own_part[c, 2] = value_parts[:rows]
 
     def soften(c):
         for j in range(NDIL):
@@ -344,7 +338,7 @@
                 total += (score[(j + 1) * half:(j + 2) * half]
                           * ahead_in[j, c, 0, at].astype(f32))
             halves.append(total.astype(bf16))
-        result = dot_nt(jnp.concatenate(halves, axis=0), weights[0])
+        result = dot_nn(jnp.concatenate(halves + [own_part[c, 0]], axis=0), weights[0])
         for j in range(NDIL):
             @pl.when(i + 2**j < n)
             def _():
@@ -361,8 +355,11 @@
                     total += (factor[(j + 1) * half:(j + 2) * half]
                               * back_in[j, c, part, at].astype(f32))
                 halves.append(total.astype(bf16))
-            result += dot_nt(jnp.concatenate(halves, axis=0), weights[1 + part])
-        out_ref[0, pl.ds(pl.multiple_of(2 * c * rows, rows), rows), :] = result.astype(bf16)
+            result += dot_nn(
+                jnp.concatenate(halves + [own_part[c, 1 + part]], axis=0), weights[1 + part])
+        out_ref[0, pl.ds(pl.multiple_of(2 * c * rows, rows), rows), :] = (
+            result[:rows].astype(bf16))
+        base[c] = result[rows:]
 
     def collect(c):
         for kind in (2, 1, 0):
@@ -382,6 +379,12 @@
         @pl.when(s + AHEAD < chunks)
         def _():
             direct(s + AHEAD)
+
+        for x, when in ((1, 0), (2, 1), (0, 2)):
+            @pl.when(s == when)
+            def _():
+                w_copies[x].wait()
+                weights[x] = stored[x].T
 
         stage(LAGS[2], attend)
         stage(LAGS[3], soften)
@@ -447,10 +450,12 @@
             pltpu.VMEM((chunks, rows, width), f32),
             pltpu.VMEM((chunks, rows, width), f32),
             pltpu.VMEM((chunks, rows, width), f32),
+            pltpu.VMEM((chunks, 3, rows, width), bf16),
             pltpu.VMEM((8 * (NDIL + 1) * rows, width), bf16),
             pltpu.VMEM((width, LANES), bf16),
             pltpu.VMEM((4, LANES, width), bf16),
             pltpu.VMEM((2, LANES, LANES), bf16),
+            pltpu.VMEM((3, width, width), bf16),
             pltpu.VMEM((3, width, width), bf16),
             dma((8, chunks)),
             dma((3,)),

time: 111 us -> 101 us (0.910)
  Pallas kernels: 109 us -> 98.5 us
    pallas_call x1, Pallas kernels: 109 us -> 98.5 us  [per_device(): pl.pallas_call(functools.partial(kernel, n, chunks, rows), out_shape=jax....]
where the time goes in v3:
time: 101 us
  Pallas kernels  98.5 us (98%)
  local copies, waits for them, and re-layouts  2.26 us (2%)
    pallas_call x1, Pallas kernels, per_device(): pl.pallas_call(functools.partial(kernel, n, chunks, rows), out_shape=jax....  98.5 us
    unnamed x1, local copies, waits for them, and re-layouts  2.26 us

profile of v3, /device:TPU:0, one launch (start us, length us, event | category | flops | bytes accessed | tf_op | source)
XLA Modules:
  0.0 100.7 jit_solution(13151345035770235109)
XLA Ops:
  0.0 98.5 %shard_map.82 = bf16[1,512,1024]{2,1,0:T(8,128)(2,1)} custom-call(s32[1,4]{1,0:T(1,128)} %links_ref.1, bf16[1,512,1024]{2,1,0:T(8,128)(2,1)} %q_ref.1, bf16[1,512,1024]{2,1,0:T(8,128)(2,1)} %k_ref.1, bf16[1,512,1024]{2,1,0:T(8,128)(2,1)} %v_ref.1, bf16[1,512,1024]{2,1,0:T(8,128)(2,1)} %g_ref.1, bf16[1024,1024]{1,0:T(8,128)(2,1)} %wq_ref.1, ...), custom_call_target="tpu_custom_call" | custom-call | tf_op jit(solution)/shard_map/pallas_call | solution.py:432
  98.5 2.3 %copy.10 = bf16[1,512,1024]{2,1,0:T(8,128)(2,1)} copy(bf16[1,512,1024]{2,1,0:T(8,128)(2,1)} %shard_map.82) | data formatting | bytes 2097152
